TPU v7x, 32 devices: a whole 2x2x4 slice. The times are simulated.
32 devices in a mesh: prow: 16 (over z, y, x), pcol: 2 (over core).
Axes of the slice: x: 2, y: 2, z: 4, core: 2. Of those that a mesh axis runs over, the one named last changes fastest.
Arguments:
- right_sides: float32 [32, 1, 4096], P(None, None, 'prow'), may hold values from -6 to 6
- factor: bfloat16 [1, 4096, 8, 512], P(None, 'prow', None, 'pcol'), as said below
- node_sizes: int32 [7], replicated, may hold values from 1 to 9, 16 in all
- row_blocks: int32 [7, 16], replicated, may hold values 0 or 1
Outputs:
- forward: float32 [32, 1, 4096], P(None, None, 'prow')
- solution: float32 [32, 8, 512], P(None, None, 'pcol')
Inputs may be any that keep to these rules, and one draw needn't show every extreme that they name: factor is zero above its diagonal; its diagonal lies between 0.5 and 1. `row_blocks`: flags of tiles that belong to no proper ancestor of the supernode are ignored.
All inputs are finite; a program needn't handle non-finite values.
Results may differ from a plain program's by a relative error of at most 0.0047.
Values may be sent and summed in bfloat16 or wider, within the bound.
A program may use at most 64 MiB of HBM per device.

v0:
```python
import jax
import jax.numpy as jnp
from jax import lax
from jax.sharding import PartitionSpec as P

LEVELS = 3


def tree_tables(node_sizes, row_blocks):
    node_count = node_sizes.shape[0]
    tile_count = row_blocks.shape[1]
    tile_ends = jnp.cumsum(node_sizes)
    tile_ids = jnp.arange(tile_count, dtype=jnp.int32)
    node_of = jnp.sum((tile_ends[None, :] <= tile_ids[:, None]).astype(jnp.int32), axis=1)
    heap_label = node_count - jnp.arange(node_count, dtype=jnp.int32)
    node_depth = jnp.zeros((node_count,), jnp.int32)
    for exponent in range(1, LEVELS):
        node_depth = node_depth + (heap_label >= 2**exponent).astype(jnp.int32)
    gap_depth = jnp.maximum(node_depth[None, :] - node_depth[:, None], 0)
    ancestor = (node_depth[:, None] < node_depth[None, :]) & (
        jnp.right_shift(heap_label[None, :], gap_depth) == heap_label[:, None]
    )
    return (node_of, node_depth, ancestor)


def lookup(source, indices, length):
    hits = indices[:, None] == jnp.arange(length, dtype=jnp.int32)[None, :]
    return jnp.sum(jnp.where(hits, source[None, :], 0), axis=1)


def rows_from_columns(factor, vector, weights):
    blocks = lax.dot_general(
        vector, factor, (((2,), (3,)), ((1,), (2,))), preferred_element_type=jnp.float32
    )
    return jnp.sum(weights.T[:, None, :, None] * blocks, axis=0)


def columns_from_rows(factor, vector, weights):
    blocks = lax.dot_general(
        vector, factor, (((2,), (1,)), ((1,), (0,))), preferred_element_type=jnp.float32
    )
    return jnp.sum(weights[:, None, :, None] * blocks, axis=0)


def to_columns(vector):
    row_count = lax.axis_size("prow")
    col_count = lax.axis_size("pcol")
    row_groups = row_count // col_count
    col_index = lax.axis_index("pcol")
    rhs_count, row_tiles, tile_rows = vector.shape
    collected = lax.all_gather(vector, "prow", axis=1, tiled=True)
    collected = collected.reshape(rhs_count, row_groups, col_count, row_tiles, tile_rows)
    picked = lax.dynamic_index_in_dim(collected, col_index, 2, keepdims=False)
    return jnp.transpose(picked, (0, 2, 1, 3)).reshape(rhs_count, row_tiles * row_groups, tile_rows)


def to_rows(vector):
    row_count = lax.axis_size("prow")
    col_count = lax.axis_size("pcol")
    row_groups = row_count // col_count
    row_index = lax.axis_index("prow")
    rhs_count, col_tiles, tile_rows = vector.shape
    shaped = vector.reshape(rhs_count, col_tiles // row_groups, row_groups, tile_rows)
    chosen = lax.dynamic_index_in_dim(shaped, row_index // col_count, 2, keepdims=False)
    collected = lax.all_gather(chosen, "pcol", axis=1, tiled=True)
    collected = collected.reshape(rhs_count, col_count, col_tiles // row_groups, tile_rows)
    return lax.dynamic_index_in_dim(collected, row_index % col_count, 1, keepdims=False)


def sum_rows(partial_value):
    return lax.psum(partial_value, "pcol")


def sum_cols(partial_value):
    return lax.psum(partial_value, "prow")


def shards(right_sides, factor, node_sizes, row_blocks):
    row_count = lax.axis_size("prow")
    col_count = lax.axis_size("pcol")
    row_index = lax.axis_index("prow")
    col_index = lax.axis_index("pcol")
    row_tiles = factor.shape[0]
    col_tiles = factor.shape[2]
    rhs_count = right_sides.shape[0]
    tile_rows = right_sides.shape[2]
    node_count = node_sizes.shape[0]
    tile_count = row_blocks.shape[1]
    node_of, node_depth, ancestor = tree_tables(node_sizes, row_blocks)
    mine_rows = jnp.arange(row_tiles, dtype=jnp.int32) * row_count + row_index
    mine_cols = jnp.arange(col_tiles, dtype=jnp.int32) * col_count + col_index
    owner_rows = lookup(node_of, mine_rows, tile_count)
    owner_cols = lookup(node_of, mine_cols, tile_count)
    depth_rows = lookup(node_depth, owner_rows, node_count)
    depth_cols = lookup(node_depth, owner_cols, node_count)
    node_ids = jnp.arange(node_count, dtype=jnp.int32)
    hits_rows = owner_rows[:, None] == node_ids[None, :]
    hits_cols = owner_cols[:, None] == node_ids[None, :]
    above = jnp.any(
        hits_rows[:, None, :, None] & ancestor[None, None, :, :] & hits_cols[None, :, None, :],
        axis=(2, 3),
    )
    tile_hits = mine_rows[:, None] == jnp.arange(tile_count, dtype=jnp.int32)[None, :]
    flagged = jnp.any(
        tile_hits[:, None, None, :]
        & hits_cols[None, :, :, None]
        & (row_blocks == 1)[None, None, :, :],
        axis=(2, 3),
    )
    diagonal = owner_rows[:, None] == owner_cols[None, :]
    linked = above & flagged
    correction = jnp.zeros(right_sides.shape, jnp.float32)
    forward = jnp.zeros(right_sides.shape, jnp.float32)
    forward_cols = jnp.zeros((rhs_count, col_tiles, tile_rows), jnp.float32)
    for height in range(LEVELS - 1, -1, -1):
        at_rows = depth_rows == height
        at_cols = depth_cols == height
        current = (right_sides - correction).astype(jnp.bfloat16)
        solve_weights = (diagonal & at_rows[:, None]).astype(jnp.float32)
        solved = sum_rows(rows_from_columns(factor, to_columns(current), solve_weights))
        forward = forward + solved
        solved_cols = to_columns(solved.astype(jnp.bfloat16))
        forward_cols = forward_cols + solved_cols.astype(jnp.float32)
        if height > 0:
            update_weights = (linked & at_cols[None, :]).astype(jnp.float32)
            correction = correction + sum_rows(
                rows_from_columns(factor, solved_cols, update_weights)
            )
    solution = jnp.zeros((rhs_count, col_tiles, tile_rows), jnp.float32)
    correction_cols = jnp.zeros((rhs_count, col_tiles, tile_rows), jnp.float32)
    for height in range(LEVELS):
        at_rows = depth_rows == height
        at_cols = depth_cols == height
        if height == 0:
            current = forward.astype(jnp.bfloat16)
        else:
            current = to_rows((forward_cols - correction_cols).astype(jnp.bfloat16))
        solve_weights = (diagonal & at_cols[None, :]).astype(jnp.float32)
        solved = sum_cols(columns_from_rows(factor, current, solve_weights))
        solution = solution + solved
        if height < LEVELS - 1:
            solved_rows = to_rows(solved.astype(jnp.bfloat16))
            update_weights = (linked & at_rows[:, None]).astype(jnp.float32)
            correction_cols = correction_cols + sum_cols(
                columns_from_rows(factor, solved_rows, update_weights)
            )
    return (forward, solution)


def solution(mesh):
    in_specs = (P(None, None, "prow"), P(None, "prow", None, "pcol"), P(), P())
    out_specs = (P(None, None, "prow"), P(None, None, "pcol"))
    return jax.shard_map(shards, mesh=mesh, in_specs=in_specs, out_specs=out_specs, check_vma=False)
```

profile of v0, /device:TPU:0, one launch (start us, length us, event | category | flops | bytes accessed | tf_op | source)
XLA Modules:
  0.0 793.3 jit_solution(14260200867232302940)
XLA Ops:
  7.3 0.9 reduce-window.8
  9.5 1.3 select_reduce_fusion.2
  14.7 43.8 %all_gather.30 = bf16[32,16,256]{2,0,1:T(8,128)(2,1)S(1)} all-gather(bf16[32,1,256]{2,0,1:T(8,128)(2,1)S(1)} %copy.112), channel_id=1, replica_groups=mesh['prow'=16,'pcol'=2] {'prow'}, dimensions={1}, use_global_device_ids=true | all-gather | bytes 278528 | tf_op jit(solution)/shard_map/all_gather | solution.py:51
  59.2 3.4 psum.70
  62.6 36.9 %all_gather.31 = bf16[32,16,256]{2,0,1:T(8,128)(2,1)S(1)} all-gather(bf16[32,1,256]{2,0,1:T(8,128)(2,1)S(1)} %convert_element_type.179), channel_id=1, replica_groups=mesh['prow'=16,'pcol'=2] {'prow'}, dimensions={1}, use_global_device_ids=true | all-gather | bytes 278528 | tf_op jit(solution)/shard_map/all_gather | solution.py:51
  99.9 3.4 psum.71
  103.3 38.9 %all_gather.32 = bf16[32,16,256]{2,0,1:T(8,128)(2,1)S(1)} all-gather(bf16[32,1,256]{2,0,1:T(8,128)(2,1)S(1)} %subtract_convert_fusion.2), channel_id=1, replica_groups=mesh['prow'=16,'pcol'=2] {'prow'}, dimensions={1}, use_global_device_ids=true | all-gather | bytes 278528 | tf_op jit(solution)/shard_map/all_gather | solution.py:51
  142.6 3.4 psum.72
  146.1 36.9 %all_gather.33 = bf16[32,16,256]{2,0,1:T(8,128)(2,1)S(1)} all-gather(bf16[32,1,256]{2,0,1:T(8,128)(2,1)S(1)} %convert_element_type.183), channel_id=1, replica_groups=mesh['prow'=16,'pcol'=2] {'prow'}, dimensions={1}, use_global_device_ids=true | all-gather | bytes 278528 | tf_op jit(solution)/shard_map/all_gather | solution.py:51
  183.4 3.4 psum.73
  186.8 39.0 %all_gather.34 = bf16[32,16,256]{2,0,1:T(8,128)(2,1)S(1)} all-gather(bf16[32,1,256]{2,0,1:T(8,128)(2,1)S(1)} %subtract_convert_fusion.1), channel_id=1, replica_groups=mesh['prow'=16,'pcol'=2] {'prow'}, dimensions={1}, use_global_device_ids=true | all-gather | bytes 278528 | tf_op jit(solution)/shard_map/all_gather | solution.py:51
  226.2 3.4 psum.74
  229.6 1.0 convolution_multiply_fusion.4
  230.7 104.0 %all-reduce.6.cloned.1.call-done = f32[32,8,256]{2,0,1:T(8,128)} async-done(((f32[32,8,256]{2,0,1:T(8,128)}), f32[32,8,256]{2,0,1:T(8,128)}) %all-reduce.6.cloned.1.call-update) | async-done | bytes 262160 | tf_op jit(solution)/shard_map/psum | solution.py:75
  334.7 0.8 dynamic-slice_convert_fusion.1
  335.5 1.8 all_gather.36
  337.3 1.0 convolution_multiply_fusion.3
  338.3 40.2 %all_gather.35 = bf16[32,16,256]{2,0,1:T(8,128)(2,1)S(1)} all-gather(bf16[32,1,256]{2,0,1:T(8,128)(2,1)S(1)} %get-tuple-element.14), channel_id=1, replica_groups=mesh['prow'=16,'pcol'=2] {'prow'}, dimensions={1}, use_global_device_ids=true | all-gather | bytes 278528 | tf_op jit(solution)/shard_map/all_gather | solution.py:51
  378.6 68.9 %all-reduce.8.cloned.1.call-done = f32[32,8,256]{2,0,1:T(8,128)} async-done(((f32[32,8,256]{2,0,1:T(8,128)}), f32[32,8,256]{2,0,1:T(8,128)}) %all-reduce.8.cloned.1.call-update) | async-done | bytes 262160 | tf_op jit(solution)/shard_map/psum | solution.py:75
  447.5 0.8 subtract_convert_fusion
  448.3 1.8 all_gather.37
  450.1 1.0 convolution_multiply_fusion.2
  451.2 108.9 %all-reduce.10.cloned.1.call-done = f32[32,8,256]{2,0,1:T(8,128)} async-done(((f32[32,8,256]{2,0,1:T(8,128)}), f32[32,8,256]{2,0,1:T(8,128)}) %all-reduce.10.cloned.1.call-update) | async-done | bytes 262160 | tf_op jit(solution)/shard_map/psum | solution.py:75
  560.8 1.8 all_gather.38
  562.7 1.0 convolution_multiply_fusion.1
  563.7 108.7 %all-reduce.12.cloned.1.call-done = f32[32,8,256]{2,0,1:T(8,128)} async-done(((f32[32,8,256]{2,0,1:T(8,128)}), f32[32,8,256]{2,0,1:T(8,128)}) %all-reduce.12.cloned.1.call-update) | async-done | bytes 262160 | tf_op jit(solution)/shard_map/psum | solution.py:75
  672.5 0.8 fusion.16
  673.3 1.8 all_gather.39
  675.1 1.0 convolution_multiply_fusion
  676.8 108.1 %all-reduce.14.cloned.1.call-done = f32[32,8,256]{2,0,1:T(8,128)} async-done(((f32[32,8,256]{2,0,1:T(8,128)}), f32[32,8,256]{2,0,1:T(8,128)}) %all-reduce.14.cloned.1.call-update) | async-done | bytes 262160 | tf_op jit(solution)/shard_map/psum | solution.py:75
  784.9 1.0 add_add_fusion
  785.9 0.9 copy.82
  (51 shorter events, 7.4 us)
Async XLA Ops:
  7.2 51.5 %copy-start = (bf16[1,256,8,256]{3,2,1,0:T(8,128)(2,1)S(1)}, bf16[1,256,8,256]{3,2,1,0:T(8,128)(2,1)}, u32[]{:S(2)}) copy-start(bf16[1,256,8,256]{3,2,1,0:T(8,128)(2,1)} %param.5) | copy-start | bytes 3145732
  7.2 7.5 copy-start.3
  7.2 327.5 %all-reduce.6.cloned.1.call-start = ((), (), s32[]{:S(2)}) async-start(), calls=%async_computation | async-start | bytes 524288 | tf_op jit(solution)/shard_map/psum | solution.py:75
  12.7 0.7 copy-start.4
  230.6 216.9 %all-reduce.8.cloned.1.call-start = ((), (), s32[]{:S(2)}) async-start(), calls=%async_computation.1 | async-start | bytes 524288 | tf_op jit(solution)/shard_map/psum | solution.py:75
  338.3 221.8 %all-reduce.10.cloned.1.call-start = ((), (), s32[]{:S(2)}) async-start(), calls=%async_computation.2 | async-start | bytes 524288 | tf_op jit(solution)/shard_map/psum | solution.py:75
  451.1 221.4 %all-reduce.12.cloned.1.call-start = ((), (), s32[]{:S(2)}) async-start(), calls=%async_computation.3 | async-start | bytes 524288 | tf_op jit(solution)/shard_map/psum | solution.py:75
  563.7 221.2 %all-reduce.14.cloned.1.call-start = ((), (), s32[]{:S(2)}) async-start(), calls=%async_computation.4 | async-start | bytes 524288 | tf_op jit(solution)/shard_map/psum | solution.py:75
  675.1 109.8 %copy-start.2 = (f32[32,8,256]{2,0,1:T(8,128)S(1)}, f32[32,8,256]{2,0,1:T(8,128)}, u32[]{:S(2)}) copy-start(f32[32,8,256]{2,0,1:T(8,128)} %all-reduce.10.cloned.1.call-done) | copy-start | bytes 786436
  676.1 108.8 %copy-start.1 = (f32[32,8,256]{2,0,1:T(8,128)S(1)}, f32[32,8,256]{2,0,1:T(8,128)}, u32[]{:S(2)}) copy-start(f32[32,8,256]{2,0,1:T(8,128)} %all-reduce.6.cloned.1.call-done) | copy-start | bytes 786436
Sparse Core Ops, SparseCore 0:
  230.8 103.9 all-reduce.5
  340.5 106.9 all-reduce.7
  453.3 106.7 all-reduce.9
  565.7 106.6 all-reduce.11
  678.1 106.7 all-reduce.13
where the time goes:
time: 794 us; the launch traced here: 793 us
  waiting for transfers between devices  499 us (63%)
  blocking collectives  260 us (33%)
  between operations  16 us (2%)
    psum x5, waiting for transfers between devices, sum_cols(): return lax.psum(partial_value, 'prow')  499 us
    all_gather x6, blocking collectives, to_columns(): collected = lax.all_gather(vector, 'prow', axis=1, tiled=True)  236 us
    psum x5, blocking collectives, sum_rows(): return lax.psum(partial_value, 'pcol')  17 us
  transfers between devices with their start and end apart: 5, of which 5 were waited for; matrix products, arithmetic and copies ran while one was open for 0% of the time, Pallas kernels for 0%

commit v1 on v0

v1 whole, which is shorter than its diff:
```python
import functools

import jax
import jax.numpy as jnp
from jax import lax
from jax.experimental import pallas as pl
from jax.experimental.pallas import tpu as pltpu
from jax.sharding import PartitionSpec as P

MESH = pl.DeviceIdType.MESH
NT_DIMS = (((1,), (1,)), ((), ()))
NN_DIMS = (((1,), (0,)), ((), ()))


def kernel(
    R, C, CT, LEVELS,
    sizes_ref, blocks_ref, b_ref, a_ref,
    fwd_ref, sol_ref,
    ag_src, ag_buf, comb_buf, rs_src, rs_buf, share_buf, fin_src, fin_buf,
    ag_send, ag_recv, comb_send, comb_recv, rs_send, rs_recv,
    share_send, share_recv, fin_send, fin_recv,
):
    SN = sizes_ref.shape[0]
    me = lax.axis_index("prow")
    col = lax.axis_index("pcol")
    mine = lax.rem(me, C) == col
    slot = me // C
    before = (me + C - 1 - col) // C
    T = b_ref.shape[2]

    ag_buf[...] = jnp.zeros_like(ag_buf)
    rs_buf[...] = jnp.zeros_like(rs_buf)

    barrier = pltpu.get_barrier_semaphore()

    def greet_row(step, carry):
        pl.semaphore_signal(
            barrier, inc=1, device_id=(lax.rem(me + step, R), col), device_id_type=MESH
        )
        return carry

    def greet_col(step, carry):
        pl.semaphore_signal(
            barrier, inc=1, device_id=(me, lax.rem(col + step, C)), device_id_type=MESH
        )
        return carry

    lax.fori_loop(1, R, greet_row, 0)
    lax.fori_loop(1, C, greet_col, 0)

    ends = []
    total = jnp.int32(0)
    for s in range(SN):
        total = total + sizes_ref[s]
        ends.append(total)

    def node_of(tile):
        count = jnp.int32(0)
        for s in range(SN):
            count = count + jnp.where(ends[s] <= tile, 1, 0)
        return jnp.minimum(count, SN - 1)

    row_node = node_of(me)
    row_label = SN - row_node
    row_level = jnp.int32(0)
    for e in range(1, LEVELS):
        row_level = row_level + jnp.where(row_label >= 2**e, 1, 0)
    same, linked = [], []
    for s in range(CT):
        node = node_of(s * C + col)
        label = SN - node
        above = jnp.int32(0)
        for gap in range(1, LEVELS):
            above = above + jnp.where(jnp.right_shift(label, gap) == row_label, 1, 0)
        flag = jnp.where(blocks_ref[node, me] == 1, 1, 0)
        same.append(node == row_node)
        linked.append(above * flag > 0)

    b = b_ref[:, 0, :]
    pl.semaphore_wait(barrier, R - 1 + C - 1)

    def ag_copy(rnd, k):
        return pltpu.make_async_remote_copy(
            src_ref=ag_src.at[rnd], dst_ref=ag_buf.at[rnd, slot],
            send_sem=ag_send.at[k], recv_sem=ag_recv.at[rnd, slot],
            device_id=(k, col), device_id_type=MESH,
        )

    def gather(rnd, value):
        @pl.when(mine)
        def _():
            if rnd > 0:
                lax.fori_loop(
                    me + 1, R, lambda k, x: (ag_copy(rnd, k).wait_send(), x)[1], 0
                )
            ag_src[rnd] = value
            lax.fori_loop(
                0, R - 1 - me, lambda k, x: (ag_copy(rnd, R - 1 - k).start(), x)[1], 0
            )
            ag_buf[rnd, slot] = value

        def arrive(s, carry):
            pltpu.make_async_remote_copy(
                src_ref=ag_src.at[rnd], dst_ref=ag_buf.at[rnd, s],
                send_sem=ag_send.at[0], recv_sem=ag_recv.at[rnd, s],
                device_id=(me, col), device_id_type=MESH,
            ).wait_recv()
            return carry

        lax.fori_loop(0, before, arrive, 0)

    def multiply(rnd, masks):
        zero = jnp.zeros((b.shape[0], T), jnp.bfloat16)
        parts = [jnp.where(masks[s], ag_buf[rnd, s], zero) for s in range(CT)]
        return lax.dot_general(
            jnp.concatenate(parts, axis=1), a_ref[...], NT_DIMS,
            preferred_element_type=jnp.float32,
        )

    def comb_copy(rnd, step):
        to = lax.rem(col + step, C)
        return pltpu.make_async_remote_copy(
            src_ref=comb_buf.at[rnd, col], dst_ref=comb_buf.at[rnd, col],
            send_sem=comb_send.at[rnd, step], recv_sem=comb_recv.at[rnd, col],
            device_id=(me, to), device_id_type=MESH,
        )

    def combine(rnd, partial):
        comb_buf[rnd, col] = partial
        for step in range(1, C):
            comb_copy(rnd, step).start()
        for step in range(1, C):
            origin = lax.rem(col + step, C)
            pltpu.make_async_remote_copy(
                src_ref=comb_buf.at[rnd, col], dst_ref=comb_buf.at[rnd, origin],
                send_sem=comb_send.at[rnd, step], recv_sem=comb_recv.at[rnd, origin],
                device_id=(me, origin), device_id_type=MESH,
            ).wait_recv()
        out = comb_buf[rnd, 0]
        for c in range(1, C):
            out = out + comb_buf[rnd, c]
        return out

    zeros = jnp.zeros(b.shape, jnp.float32)
    forward = zeros
    correction = zeros
    rnd = 0
    for level in range(LEVELS - 1, -1, -1):
        here = row_level == level
        gather(rnd, (b - correction).astype(jnp.bfloat16))
        solved = combine(rnd, multiply(rnd, same))
        solved = jnp.where(here, solved, zeros)
        forward = forward + solved
        rnd += 1
        if level > 0:
            gather(rnd, solved.astype(jnp.bfloat16))
            correction = correction + combine(rnd, multiply(rnd, linked))
            rnd += 1
    fwd_ref[:, 0, :] = forward
    rounded = forward.astype(jnp.bfloat16)
    base = rounded.astype(jnp.float32)

    def rs_copy(rnd, s):
        return pltpu.make_async_remote_copy(
            src_ref=rs_src.at[rnd, s], dst_ref=rs_buf.at[rnd, me],
            send_sem=rs_send.at[rnd, s], recv_sem=rs_recv.at[rnd, me],
            device_id=(s * C + col, col), device_id_type=MESH,
        )

    def scatter(rnd, value, masks):
        blocks = lax.dot_general(
            value, a_ref[...], NN_DIMS, preferred_element_type=jnp.float32
        )
        for s in range(CT):
            rs_src[rnd, s] = jnp.where(
                masks[s], blocks[:, s * T:(s + 1) * T], zeros
            ).astype(jnp.bfloat16)
        lax.fori_loop(0, before, lambda s, x: (rs_copy(rnd, s).start(), x)[1], 0)

    def reduce(rnd):
        def arrive(k, carry):
            pltpu.make_async_remote_copy(
                src_ref=rs_src.at[rnd, 0], dst_ref=rs_buf.at[rnd, k],
                send_sem=rs_send.at[rnd, 0], recv_sem=rs_recv.at[rnd, k],
                device_id=(k, col), device_id_type=MESH,
            ).wait_recv()
            return carry

        lax.fori_loop(me + 1, R, arrive, 0)
        out = rs_src[rnd, slot].astype(jnp.float32)
        for k in range(R):
            out = out + rs_buf[rnd, k].astype(jnp.float32)
        return out

    def share_copy(rnd, step):
        return pltpu.make_async_remote_copy(
            src_ref=share_buf.at[rnd], dst_ref=share_buf.at[rnd],
            send_sem=share_send.at[rnd, step], recv_sem=share_recv.at[rnd],
            device_id=(me, lax.rem(col + step, C)), device_id_type=MESH,
        )

    def share(rnd, finish):
        @pl.when(mine)
        def _():
            share_buf[rnd] = finish(reduce(rnd))
            for step in range(1, C):
                share_copy(rnd, step).start()

        if C > 1:
            @pl.when(jnp.logical_not(mine))
            def _():
                share_copy(rnd, 1).wait_recv()

        return share_buf[rnd]

    fin_src[...] = zeros
    update = zeros
    rnd = 0
    current = jnp.where(row_level == 0, rounded, jnp.zeros_like(rounded))
    for level in range(LEVELS):
        scatter(rnd, current, same)
        if level < LEVELS - 1:
            def keep(value):
                fin_src[...] = fin_src[...] + value
                return value

            solved = share(rnd, keep).astype(jnp.bfloat16)
            rnd += 1
            scatter(rnd, solved, linked)
            update = update + share(rnd, lambda value: value)
            rnd += 1
            current = jnp.where(
                row_level == level + 1, base - update, zeros
            ).astype(jnp.bfloat16)

    def fin_copy(step):
        return pltpu.make_async_remote_copy(
            src_ref=fin_buf.at[slot], dst_ref=fin_buf.at[slot],
            send_sem=fin_send.at[step], recv_sem=fin_recv.at[slot],
            device_id=(lax.rem(me + step, R), col), device_id_type=MESH,
        )

    @pl.when(mine)
    def _():
        fin_buf[slot] = (fin_src[...] + reduce(rnd)).astype(jnp.bfloat16)
        lax.fori_loop(1, R, lambda step, x: (fin_copy(step).start(), x)[1], 0)

    def fin_arrive(s, carry):
        @pl.when(s * C + col != me)
        def _():
            pltpu.make_async_remote_copy(
                src_ref=fin_buf.at[s], dst_ref=fin_buf.at[s],
                send_sem=fin_send.at[0], recv_sem=fin_recv.at[s],
                device_id=(me, col), device_id_type=MESH,
            ).wait_recv()
        return carry

    for r in range(comb_buf.shape[0]):
        for step in range(1, C):
            comb_copy(r, step).wait_send()
    for r in range(rs_buf.shape[0]):
        lax.fori_loop(0, before, lambda s, x: (rs_copy(r, s).wait_send(), x)[1], 0)

    @pl.when(mine)
    def _():
        lax.fori_loop(me + 1, R, lambda k, x: (ag_copy(0, k).wait_send(), x)[1], 0)
        for r in range(share_buf.shape[0]):
            for step in range(1, C):
                share_copy(r, step).wait_send()

    lax.fori_loop(0, CT, fin_arrive, 0)
    for s in range(CT):
        sol_ref[:, s, :] = fin_buf[s].astype(jnp.float32)

    @pl.when(mine)
    def _():
        lax.fori_loop(1, R, lambda step, x: (fin_copy(step).wait_send(), x)[1], 0)


def shards(R, C, right_sides, factor, node_sizes, row_blocks):
    rhs, row_tiles, T = right_sides.shape
    rows, CT = factor.shape[1], factor.shape[2]
    levels = (node_sizes.shape[0] + 1).bit_length() - 1
    assert row_tiles == 1 and rows == T and CT * C == R
    rounds = 2 * levels - 1
    matrix = factor.reshape(rows, CT * T)
    vmem = pl.BlockSpec(memory_space=pltpu.VMEM)
    smem = pl.BlockSpec(memory_space=pltpu.SMEM)
    dma = pltpu.SemaphoreType.DMA
    bf16, f32 = jnp.bfloat16, jnp.float32
    return pl.pallas_call(
        functools.partial(kernel, R, C, CT, levels),
        out_shape=(
            jax.ShapeDtypeStruct((rhs, 1, T), f32),
            jax.ShapeDtypeStruct((rhs, CT, T), f32),
        ),
        in_specs=[smem, smem, vmem, vmem],
        out_specs=(vmem, vmem),
        scratch_shapes=[
            pltpu.VMEM((rounds, rhs, T), bf16),
            pltpu.VMEM((rounds, CT, rhs, T), bf16),
            pltpu.VMEM((rounds, C, rhs, T), f32),
            pltpu.VMEM((rounds, CT, rhs, T), bf16),
            pltpu.VMEM((rounds, R, rhs, T), bf16),
            pltpu.VMEM((rounds - 1, rhs, T), f32),
            pltpu.VMEM((rhs, T), f32),
            pltpu.VMEM((CT, rhs, T), bf16),
            dma((R,)),
            dma((rounds, CT)),
            dma((rounds, C)),
            dma((rounds, C)),
            dma((rounds, CT)),
            dma((rounds, R)),
            dma((rounds - 1, C)),
            dma((rounds - 1,)),
            dma((R,)),
            dma((CT,)),
        ],
        compiler_params=pltpu.CompilerParams(collective_id=0, has_side_effects=True),
        name="tree_solve",
    )(node_sizes, row_blocks, right_sides, matrix)


def solution(mesh):
    in_specs = (P(None, None, "prow"), P(None, "prow", None, "pcol"), P(), P())
    out_specs = (P(None, None, "prow"), P(None, None, "pcol"))
    body = functools.partial(shards, mesh.shape["prow"], mesh.shape["pcol"])
    return jax.shard_map(
        body, mesh=mesh, in_specs=in_specs, out_specs=out_specs, check_vma=False
    )
```

time: 794 us -> 75.4 us (0.09)
  waiting for transfers between devices: 499 us -> 0 us
  blocking collectives: 260 us -> 0 us
  Pallas kernels: 0 us -> 68.9 us
  between operations: 16 us -> 0.64 us
    psum x5 -> x0, waiting for transfers between devices: 499 us -> none  [sum_cols(): return lax.psum(partial_value, 'prow')]
    all_gather x10 -> x0, blocking collectives: 243 us -> none  [the longest x6 236 us: to_columns(): collected = lax.all_gather(vector, 'prow', axis=1, tiled=True)]
    pallas_call x0 -> x1, Pallas kernels: none -> 68.9 us  [shards(): pl.pallas_call(functools.partial(kernel, R, C, CT, levels), out_shape=(ja...]
    psum x5 -> x0, blocking collectives: 17 us -> none  [sum_rows(): return lax.psum(partial_value, 'pcol')]
  transfers between devices with their start and end apart: 5 -> 0, of which waited for: 5 -> 0; matrix products, arithmetic and copies ran while one was open for 0% -> 0% of each run, Pallas kernels for 0% -> 0%
where the time goes in v1:
time: 75.4 us; the launch traced here: 75.1 us
  Pallas kernels  68.9 us (91%)
  local copies, waits for them, and re-layouts  5.56 us (7%)
    pallas_call x1, Pallas kernels, shards(): pl.pallas_call(functools.partial(kernel, R, C, CT, levels), out_shape=(ja...  68.9 us
    unnamed x3, local copies, waits for them, and re-layouts  5.56 us

profile of v1, /device:TPU:0, one launch (start us, length us, event | category | flops | bytes accessed | tf_op | source)
XLA Modules:
  0.0 75.1 jit_solution(18338747140156583747)
XLA Ops:
  0.6 2.5 %copy.6 = bf16[32,8,8,256]{3,1,2,0:T(8,128)(2,1)} copy(bf16[32,8,8,256]{3,2,1,0:T(8,128)(2,1)} %bitcast.4) | data formatting | bytes 2097152
  3.2 68.9 %tree_solve.1 = (f32[32,1,256]{2,1,0:T(1,128)}, f32[32,8,256]{2,1,0:T(8,128)}) custom-call(s32[7]{0:T(128)} %sizes_ref.1, s32[7,16]{1,0:T(8,128)} %blocks_ref.1, f32[32,1,256]{2,1,0:T(1,128)} %b_ref.1, bf16[256,2048]{1,0:T(8,128)(2,1)} %bitcast.3), custom_call_target="tpu_custom_call" | custom-call | tf_op jit(solution)/shard_map/tree_solve/pallas_call | solution.py:291
  72.1 1.4 %copy.9 = f32[32,1,256]{2,1,0:T(1,128)} copy(f32[32,1,256]{2,1,0:T(1,128)} %get-tuple-element.4) | data formatting | bytes 65536
  73.4 1.7 %copy.10 = f32[32,8,256]{2,1,0:T(8,128)} copy(f32[32,8,256]{2,1,0:T(8,128)} %get-tuple-element.5) | data formatting | bytes 524288

commit v2 on v1

--- a/solution.py
+++ b/solution.py
@@ -9,16 +9,21 @@
 
 MESH = pl.DeviceIdType.MESH
 NT_DIMS = (((1,), (1,)), ((), ()))
+GROUP = 2
+SPLIT = 2
+CHUNK = 64
+LANES = 128
 NN_DIMS = (((1,), (0,)), ((), ()))
 
 
 def kernel(
     R, C, CT, LEVELS,
-    sizes_ref, blocks_ref, b_ref, a_ref,
+    sizes_ref, blocks_ref, b_ref, factor_ref,
     fwd_ref, sol_ref,
-    ag_src, ag_buf, comb_buf, rs_src, rs_buf, share_buf, fin_src, fin_buf,
+    raw, wide, a_ref,
+    ag_src, ag_buf, comb_buf, rs_src, rs_buf, share_buf, fin_src, fin_buf, update,
     ag_send, ag_recv, comb_send, comb_recv, rs_send, rs_recv,
-    share_send, share_recv, fin_send, fin_recv,
+    share_send, share_recv, fin_send, fin_recv, load_sem,
 ):
     SN = sizes_ref.shape[0]
     me = lax.axis_index("prow")
@@ -28,9 +33,8 @@
     before = (me + C - 1 - col) // C
     T = b_ref.shape[2]
 
-    ag_buf[...] = jnp.zeros_like(ag_buf)
-    rs_buf[...] = jnp.zeros_like(rs_buf)
-
+    load = pltpu.make_async_copy(factor_ref.at[0], raw, load_sem)
+    load.start()
     barrier = pltpu.get_barrier_semaphore()
 
     def greet_row(step, carry):
@@ -73,11 +77,25 @@
         for gap in range(1, LEVELS):
             above = above + jnp.where(jnp.right_shift(label, gap) == row_label, 1, 0)
         flag = jnp.where(blocks_ref[node, me] == 1, 1, 0)
-        same.append(node == row_node)
-        linked.append(above * flag > 0)
+        low = jnp.where(s * C + col <= me, 1, 0)
+        same.append(jnp.where(node == row_node, 1, 0) * low > 0)
+        linked.append(above * flag * low > 0)
 
     b = b_ref[:, 0, :]
     pl.semaphore_wait(barrier, R - 1 + C - 1)
+
+    def relayout(step, carry):
+        start = pl.multiple_of(step * CHUNK, CHUNK)
+        rows = pl.ds(start, CHUNK)
+        for h in range(T // LANES):
+            block = raw[rows, :, h * LANES:(h + 1) * LANES].astype(jnp.float32)
+            wide[h] = block.reshape(CHUNK * CT, LANES)
+        for s in range(CT):
+            for h in range(T // LANES):
+                part = wide[h, pl.ds(s, CHUNK, stride=CT), :]
+                at = s * T + h * LANES
+                a_ref[rows, at:at + LANES] = part.astype(jnp.bfloat16)
+        return carry
 
     def ag_copy(rnd, k):
         return pltpu.make_async_remote_copy(
@@ -86,7 +104,7 @@
             device_id=(k, col), device_id_type=MESH,
         )
 
-    def gather(rnd, value):
+    def send_row(rnd, value):
         @pl.when(mine)
         def _():
             if rnd > 0:
@@ -95,27 +113,31 @@
                 )
             ag_src[rnd] = value
             lax.fori_loop(
-                0, R - 1 - me, lambda k, x: (ag_copy(rnd, R - 1 - k).start(), x)[1], 0
+                me + 1, R, lambda k, x: (ag_copy(rnd, k).start(), x)[1], 0
             )
             ag_buf[rnd, slot] = value
 
-        def arrive(s, carry):
-            pltpu.make_async_remote_copy(
-                src_ref=ag_src.at[rnd], dst_ref=ag_buf.at[rnd, s],
-                send_sem=ag_send.at[0], recv_sem=ag_recv.at[rnd, s],
-                device_id=(me, col), device_id_type=MESH,
-            ).wait_recv()
-            return carry
-
-        lax.fori_loop(0, before, arrive, 0)
+    def arrive_at(rnd, s):
+        pltpu.make_async_remote_copy(
+            src_ref=ag_src.at[rnd], dst_ref=ag_buf.at[rnd, s],
+            send_sem=ag_send.at[0], recv_sem=ag_recv.at[rnd, s],
+            device_id=(me, col), device_id_type=MESH,
+        ).wait_recv()
 
     def multiply(rnd, masks):
         zero = jnp.zeros((b.shape[0], T), jnp.bfloat16)
-        parts = [jnp.where(masks[s], ag_buf[rnd, s], zero) for s in range(CT)]
-        return lax.dot_general(
-            jnp.concatenate(parts, axis=1), a_ref[...], NT_DIMS,
-            preferred_element_type=jnp.float32,
-        )
+        out = None
+        for last in range(CT, 0, -GROUP):
+            group = range(max(last - GROUP, 0), last)
+            for s in reversed(group):
+                pl.when(s < before)(functools.partial(arrive_at, rnd, s))
+            parts = [jnp.where(masks[s], ag_buf[rnd, s], zero) for s in group]
+            value = lax.dot_general(
+                jnp.concatenate(parts, axis=1), a_ref[:, group[0] * T:last * T], NT_DIMS,
+                preferred_element_type=jnp.float32,
+            )
+            out = value if out is None else out + value
+        return out
 
     def comb_copy(rnd, step):
         to = lax.rem(col + step, C)
@@ -147,16 +169,19 @@
     rnd = 0
     for level in range(LEVELS - 1, -1, -1):
         here = row_level == level
-        gather(rnd, (b - correction).astype(jnp.bfloat16))
+        send_row(rnd, (b - correction).astype(jnp.bfloat16))
+        if rnd == 0:
+            load.wait()
+            lax.fori_loop(0, T // CHUNK, relayout, 0)
         solved = combine(rnd, multiply(rnd, same))
         solved = jnp.where(here, solved, zeros)
         forward = forward + solved
         rnd += 1
         if level > 0:
-            gather(rnd, solved.astype(jnp.bfloat16))
+            send_row(rnd, solved.astype(jnp.bfloat16))
             correction = correction + combine(rnd, multiply(rnd, linked))
             rnd += 1
-    fwd_ref[:, 0, :] = forward
+    fwd_ref[...] = forward
     rounded = forward.astype(jnp.bfloat16)
     base = rounded.astype(jnp.float32)
 
@@ -168,14 +193,17 @@
         )
 
     def scatter(rnd, value, masks):
-        blocks = lax.dot_general(
-            value, a_ref[...], NN_DIMS, preferred_element_type=jnp.float32
-        )
-        for s in range(CT):
-            rs_src[rnd, s] = jnp.where(
-                masks[s], blocks[:, s * T:(s + 1) * T], zeros
-            ).astype(jnp.bfloat16)
-        lax.fori_loop(0, before, lambda s, x: (rs_copy(rnd, s).start(), x)[1], 0)
+        for last in range(CT, 0, -SPLIT):
+            first = max(last - SPLIT, 0)
+            blocks = lax.dot_general(
+                value, a_ref[:, first * T:last * T], NN_DIMS,
+                preferred_element_type=jnp.float32,
+            )
+            for s in reversed(range(first, last)):
+                rs_src[rnd, s] = jnp.where(
+                    masks[s], blocks[:, (s - first) * T:(s - first + 1) * T], zeros
+                ).astype(jnp.bfloat16)
+                pl.when(s < before)(rs_copy(rnd, s).start)
 
     def reduce(rnd):
         def arrive(k, carry):
@@ -184,13 +212,9 @@
                 send_sem=rs_send.at[rnd, 0], recv_sem=rs_recv.at[rnd, k],
                 device_id=(k, col), device_id_type=MESH,
             ).wait_recv()
-            return carry
-
-        lax.fori_loop(me + 1, R, arrive, 0)
-        out = rs_src[rnd, slot].astype(jnp.float32)
-        for k in range(R):
-            out = out + rs_buf[rnd, k].astype(jnp.float32)
-        return out
+            return carry + rs_buf[rnd, k].astype(jnp.float32)
+
+        return lax.fori_loop(me + 1, R, arrive, rs_src[rnd, slot].astype(jnp.float32))
 
     def share_copy(rnd, step):
         return pltpu.make_async_remote_copy(
@@ -202,7 +226,7 @@
     def share(rnd, finish):
         @pl.when(mine)
         def _():
-            share_buf[rnd] = finish(reduce(rnd))
+            share_buf[rnd] = finish(reduce(rnd)).astype(jnp.bfloat16)
             for step in range(1, C):
                 share_copy(rnd, step).start()
 
@@ -214,24 +238,27 @@
         return share_buf[rnd]
 
     fin_src[...] = zeros
-    update = zeros
+    update[...] = zeros
     rnd = 0
     current = jnp.where(row_level == 0, rounded, jnp.zeros_like(rounded))
-    for level in range(LEVELS):
+    for level in range(LEVELS - 1):
         scatter(rnd, current, same)
-        if level < LEVELS - 1:
-            def keep(value):
-                fin_src[...] = fin_src[...] + value
-                return value
-
-            solved = share(rnd, keep).astype(jnp.bfloat16)
-            rnd += 1
-            scatter(rnd, solved, linked)
-            update = update + share(rnd, lambda value: value)
-            rnd += 1
-            current = jnp.where(
-                row_level == level + 1, base - update, zeros
-            ).astype(jnp.bfloat16)
+
+        def keep(value):
+            fin_src[...] = fin_src[...] + value
+            return value
+
+        solved = share(rnd, keep)
+        rnd += 1
+        scatter(rnd, solved, linked)
+
+        def settle(value):
+            update[...] = update[...] + value
+            return jnp.where(row_level == level + 1, base - update[...], zeros)
+
+        current = share(rnd, settle)
+        rnd += 1
+    scatter(rnd, current, same)
 
     def fin_copy(step):
         return pltpu.make_async_remote_copy(
@@ -270,11 +297,17 @@
 
     lax.fori_loop(0, CT, fin_arrive, 0)
     for s in range(CT):
-        sol_ref[:, s, :] = fin_buf[s].astype(jnp.float32)
+        sol_ref[s] = fin_buf[s]
 
     @pl.when(mine)
     def _():
         lax.fori_loop(1, R, lambda step, x: (fin_copy(step).wait_send(), x)[1], 0)
+
+
+def finish_kernel(rows_ref, tiles_ref, fwd_ref, sol_ref):
+    fwd_ref[:, 0, :] = rows_ref[...]
+    for s in range(tiles_ref.shape[0]):
+        sol_ref[:, s, :] = tiles_ref[s].astype(jnp.float32)
 
 
 def shards(R, C, right_sides, factor, node_sizes, row_blocks):
@@ -283,28 +316,31 @@
     levels = (node_sizes.shape[0] + 1).bit_length() - 1
     assert row_tiles == 1 and rows == T and CT * C == R
     rounds = 2 * levels - 1
-    matrix = factor.reshape(rows, CT * T)
     vmem = pl.BlockSpec(memory_space=pltpu.VMEM)
     smem = pl.BlockSpec(memory_space=pltpu.SMEM)
     dma = pltpu.SemaphoreType.DMA
     bf16, f32 = jnp.bfloat16, jnp.float32
-    return pl.pallas_call(
+    forward, tiles = pl.pallas_call(
         functools.partial(kernel, R, C, CT, levels),
         out_shape=(
-            jax.ShapeDtypeStruct((rhs, 1, T), f32),
-            jax.ShapeDtypeStruct((rhs, CT, T), f32),
+            jax.ShapeDtypeStruct((rhs, T), f32),
+            jax.ShapeDtypeStruct((CT, rhs, T), bf16),
         ),
-        in_specs=[smem, smem, vmem, vmem],
+        in_specs=[smem, smem, vmem, pl.BlockSpec(memory_space=pl.ANY)],
         out_specs=(vmem, vmem),
         scratch_shapes=[
+            pltpu.VMEM((rows, CT, T), bf16),
+            pltpu.VMEM((T // LANES, CHUNK * CT, LANES), f32),
+            pltpu.VMEM((rows, CT * T), bf16),
             pltpu.VMEM((rounds, rhs, T), bf16),
             pltpu.VMEM((rounds, CT, rhs, T), bf16),
             pltpu.VMEM((rounds, C, rhs, T), f32),
             pltpu.VMEM((rounds, CT, rhs, T), bf16),
             pltpu.VMEM((rounds, R, rhs, T), bf16),
-            pltpu.VMEM((rounds - 1, rhs, T), f32),
+            pltpu.VMEM((rounds - 1, rhs, T), bf16),
             pltpu.VMEM((rhs, T), f32),
             pltpu.VMEM((CT, rhs, T), bf16),
+            pltpu.VMEM((rhs, T), f32),
             dma((R,)),
             dma((rounds, CT)),
             dma((rounds, C)),
@@ -315,10 +351,22 @@
             dma((rounds - 1,)),
             dma((R,)),
             dma((CT,)),
+            dma,
         ],
         compiler_params=pltpu.CompilerParams(collective_id=0, has_side_effects=True),
         name="tree_solve",
-    )(node_sizes, row_blocks, right_sides, matrix)
+    )(node_sizes, row_blocks, right_sides, factor)
+
+    return pl.pallas_call(
+        finish_kernel,
+        out_shape=(
+            jax.ShapeDtypeStruct((rhs, 1, T), f32),
+            jax.ShapeDtypeStruct((rhs, CT, T), f32),
+        ),
+        in_specs=[vmem, vmem],
+        out_specs=(vmem, vmem),
+        name="place",
+    )(forward, tiles)
 
 
 def solution(mesh):

time: 75.4 us -> 67.4 us (0.89)
  local copies, waits for them, and re-layouts: 5.56 us -> 0 us
  Pallas kernels: 68.9 us -> 66.5 us
    unnamed x3 -> x0, local copies, waits for them, and re-layouts: 5.56 us -> none
    pallas_call x1, Pallas kernels: 68.9 us -> 64.8 us  [shards(): pl.pallas_call(functools.partial(kernel, R, C, CT, levels), out_shape=(ja...]
    pallas_call x0 -> x1, Pallas kernels: none -> 1.72 us  [shards(): pl.pallas_call(finish_kernel, out_shape=(jax.ShapeDtypeStruct((rhs, 1, T)...]
where the time goes in v2:
time: 67.4 us; the launch traced here: 67.2 us
  Pallas kernels  66.5 us (99%)
    pallas_call x1, Pallas kernels, shards(): pl.pallas_call(functools.partial(kernel, R, C, CT, levels), out_shape=(ja...  64.8 us
    pallas_call x1, Pallas kernels, shards(): pl.pallas_call(finish_kernel, out_shape=(jax.ShapeDtypeStruct((rhs, 1, T)...  1.72 us

profile of v2, /device:TPU:0, one launch (start us, length us, event | category | flops | bytes accessed | tf_op | source)
XLA Modules:
  0.0 67.2 jit_solution(17804197624592915438)
XLA Ops:
  0.6 64.8 %tree_solve.1 = (f32[32,256]{1,0:T(8,128)}, bf16[8,32,256]{2,1,0:T(8,128)(2,1)}) custom-call(s32[7]{0:T(128)} %sizes_ref.1, s32[7,16]{1,0:T(8,128)} %blocks_ref.1, f32[32,1,256]{2,1,0:T(1,128)} %b_ref.1, bf16[1,256,8,256]{3,2,1,0:T(8,128)(2,1)} %factor_ref.1), custom_call_target="tpu_custom_call" | custom-call | tf_op jit(solution)/shard_map/tree_solve/pallas_call | solution.py:323
  65.4 1.7 %place.1 = (f32[32,1,256]{2,1,0:T(1,128)}, f32[32,8,256]{2,1,0:T(8,128)}) custom-call(f32[32,256]{1,0:T(8,128)} %get-tuple-element.4.rows_ref, bf16[8,32,256]{2,1,0:T(8,128)(2,1)} %get-tuple-element.5.tiles_ref), custom_call_target="tpu_custom_call" | custom-call | tf_op jit(solution)/shard_map/place/pallas_call | solution.py:360

commit v3 on v2

--- a/solution.py
+++ b/solution.py
@@ -10,7 +10,7 @@
 MESH = pl.DeviceIdType.MESH
 NT_DIMS = (((1,), (1,)), ((), ()))
 GROUP = 2
-SPLIT = 2
+SPLIT = 8
 CHUNK = 64
 LANES = 128
 NN_DIMS = (((1,), (0,)), ((), ()))

time: 67.4 us -> 66.8 us (level)
  no operation moved by 1% of the time
where the time goes in v3:
time: 66.8 us; the launch traced here: 66.6 us
  Pallas kernels  66 us (99%)
    pallas_call x1, Pallas kernels, shards(): pl.pallas_call(functools.partial(kernel, R, C, CT, levels), out_shape=(ja...  64.3 us
    pallas_call x1, Pallas kernels, shards(): pl.pallas_call(finish_kernel, out_shape=(jax.ShapeDtypeStruct((rhs, 1, T)...  1.72 us

profile of v3, /device:TPU:0, one launch (start us, length us, event | category | flops | bytes accessed | tf_op | source)
XLA Modules:
  0.0 66.6 jit_solution(8898816475294856831)
XLA Ops:
  0.6 64.3 %tree_solve.1 = (f32[32,256]{1,0:T(8,128)}, bf16[8,32,256]{2,1,0:T(8,128)(2,1)}) custom-call(s32[7]{0:T(128)} %sizes_ref.1, s32[7,16]{1,0:T(8,128)} %blocks_ref.1, f32[32,1,256]{2,1,0:T(1,128)} %b_ref.1, bf16[1,256,8,256]{3,2,1,0:T(8,128)(2,1)} %factor_ref.1), custom_call_target="tpu_custom_call" | custom-call | tf_op jit(solution)/shard_map/tree_solve/pallas_call | solution.py:323
  64.9 1.7 %place.1 = (f32[32,1,256]{2,1,0:T(1,128)}, f32[32,8,256]{2,1,0:T(8,128)}) custom-call(f32[32,256]{1,0:T(8,128)} %get-tuple-element.4.rows_ref, bf16[8,32,256]{2,1,0:T(8,128)(2,1)} %get-tuple-element.5.tiles_ref), custom_call_target="tpu_custom_call" | custom-call | tf_op jit(solution)/shard_map/place/pallas_call | solution.py:360
